TPU v7x, 32 devices: a whole 2x2x4 slice. The times are simulated.
32 devices in a mesh: band: 4 (over y, core), lev: 8 (over z, x).
Axes of the slice: x: 2, y: 2, z: 4, core: 2. Of those that a mesh axis runs over, the one named last changes fastest.
Arguments:
- azimuthal_coeffs: bfloat16 [2560, 64, 64], P('band', 'lev'), may hold values from -6 to 6
- polynomial_tables: bfloat16 [32, 2, 448, 1280], P(('band', 'lev')), may hold values from -0.15625 to 0.15625
- gauss_masses: float32 [1280], replicated, may hold values from 0.3 to 1.5
- circle_samples: int32 [1280], replicated, may hold values from 20 to 152, as said below
- table_lookup: int32 [32], replicated, may hold values from 0 to 31, each once
- eigen_basis: float32 [16, 16], replicated, may hold values from -1.5 to 1.5
- basis_mapping: float32 [16, 16], replicated, may hold values from -1.5 to 1.5
- eigen_constants: float32 [16], replicated, may hold values from 0.5 to 2
- hydrostatic_matrix: float32 [16, 16], replicated, may hold values from -1.5 to 1.5
- thermal_response: float32 [16, 16], replicated, may hold values from -1.5 to 1.5
Outputs:
- advanced: bfloat16 [2560, 64, 64], P('band', 'lev')
Inputs may be any that keep to these rules, and one draw needn't show every extreme that they name: circle_samples[j] is 20 + 4 * floor(j * 32 / 1280) plus 0, 4 or 8; row 0 holds 20 and row 1279 the largest value. table_lookup is a permutation of 0 .. 31.
All inputs are finite; a program needn't handle non-finite values.
Results may differ from a plain program's by a relative error of at most 0.0041.
The roundings to bfloat16 on the way count: a program that leaves them out, or rounds other values in their place, can miss the bound.
Values may be sent and summed in bfloat16 or wider, within the bound.
No kernel may reach another device: no remote copies, remote signals or barrier semaphores. Data moves between devices by JAX's collectives and lax.ppermute only.
A program may use at most 64 MiB of HBM per device.

v0:
```python
import jax
import jax.numpy as jnp
from jax import lax
from jax.sharding import PartitionSpec as P

TRUNC = 1280
FIELDS = 4
TRUNCATION_LIMIT = lax.Precision.HIGHEST
STIFFNESS = 8.0
DIFFUSION = 4.0


def harmonic_advance(
    harmonic_current,
    total_order,
    eigen_basis,
    basis_mapping,
    eigen_constants,
    hydrostatic_matrix,
    thermal_response,
):
    scaled = total_order * (total_order + 1.0) / (TRUNC * (TRUNC + 1.0))
    implicit_weighting = STIFFNESS * scaled
    rotational_curl = harmonic_current[:, 0]
    dilatation_current = harmonic_current[:, 1]
    thermal_current = harmonic_current[:, 2]
    moisture = harmonic_current[:, 3]
    hyper_viscosity = 1.0 / (1.0 + DIFFUSION * scaled * scaled)
    explicit_righthand = dilatation_current + implicit_weighting[:, None, None] * jnp.einsum(
        "li,eic->elc", hydrostatic_matrix, thermal_current, precision=TRUNCATION_LIMIT
    )
    projected = jnp.einsum(
        "li,eic->elc", basis_mapping, explicit_righthand, precision=TRUNCATION_LIMIT
    )
    projected = projected / (
        1.0 + implicit_weighting[:, None, None] * eigen_constants[None, :, None]
    )
    dilatation_future = jnp.einsum(
        "li,eic->elc", eigen_basis, projected, precision=TRUNCATION_LIMIT
    )
    thermal_future = thermal_current - jnp.einsum(
        "li,eic->elc", thermal_response, dilatation_future, precision=TRUNCATION_LIMIT
    )
    return jnp.stack(
        [
            rotational_curl * hyper_viscosity[:, None, None],
            dilatation_future,
            thermal_future,
            moisture * hyper_viscosity[:, None, None],
        ],
        axis=1,
    )


def analyse_wave(column, zonal_order, operator_array, gauss_masses, circle_samples):
    half_rows = operator_array.shape[2]
    live_mask = (2 * zonal_order < circle_samples).astype(jnp.float32)
    north = column[:half_rows].astype(jnp.float32)
    south = jnp.flip(column[half_rows:], axis=0).astype(jnp.float32)
    weight_col = (gauss_masses * live_mask)[:, None]
    even_part = ((north + south) * weight_col).astype(jnp.bfloat16)
    odd_part = ((north - south) * weight_col).astype(jnp.bfloat16)
    spec_even = jnp.dot(operator_array[0], even_part, preferred_element_type=jnp.float32)
    spec_odd = jnp.dot(operator_array[1], odd_part, preferred_element_type=jnp.float32)
    return jnp.stack([spec_even, spec_odd], axis=0)


def complete_harmonic(
    harmonic_coeffs,
    zonal_order,
    operator_array,
    circle_samples,
    eigen_basis,
    basis_mapping,
    eigen_constants,
    hydrostatic_matrix,
    thermal_response,
):
    pair_rows = harmonic_coeffs.shape[1]
    col_count = harmonic_coeffs.shape[2]
    offsets = jnp.arange(pair_rows, dtype=jnp.int32) * 2 + zonal_order
    keep_even = (offsets < TRUNC).astype(jnp.float32)[:, None]
    keep_odd = (offsets + 1 < TRUNC).astype(jnp.float32)[:, None]
    harmonic_current = jnp.concatenate(
        [harmonic_coeffs[0] * keep_even, harmonic_coeffs[1] * keep_odd], axis=0
    )
    total_order = jnp.concatenate([offsets, offsets + 1]).astype(jnp.float32)
    arranged = harmonic_current.reshape(2 * pair_rows, FIELDS, col_count // (2 * FIELDS), 2)
    refreshed = harmonic_advance(
        arranged,
        total_order,
        eigen_basis,
        basis_mapping,
        eigen_constants,
        hydrostatic_matrix,
        thermal_response,
    )
    refreshed = refreshed.reshape(2 * pair_rows, col_count).astype(jnp.bfloat16)
    contract = (((0,), (0,)), ((), ()))
    even_sum = lax.dot_general(
        operator_array[0], refreshed[:pair_rows], contract, preferred_element_type=jnp.float32
    )
    odd_sum = lax.dot_general(
        operator_array[1], refreshed[pair_rows:], contract, preferred_element_type=jnp.float32
    )
    live_col = (2 * zonal_order < circle_samples).astype(jnp.float32)[:, None]
    north_out = (even_sum + odd_sum) * live_col
    south_out = (even_sum - odd_sum) * live_col
    return jnp.concatenate([north_out, jnp.flip(south_out, axis=0)], axis=0).astype(jnp.bfloat16)


def per_device(
    azimuthal_coeffs,
    polynomial_tables,
    gauss_masses,
    circle_samples,
    table_lookup,
    eigen_basis,
    basis_mapping,
    eigen_constants,
    hydrostatic_matrix,
    thermal_response,
):
    lat_rows, level_cols, last_width = azimuthal_coeffs.shape
    wave_count = last_width // 2
    band_count = lax.axis_size("band")
    lev_count = lax.axis_size("lev")
    device_id = lax.axis_index("band") * lev_count + lax.axis_index("lev")
    serial = jnp.arange(wave_count, dtype=jnp.int32)
    wave_of = jnp.zeros((wave_count,), jnp.int32).at[table_lookup].set(serial)
    own_wave = jnp.sum(jnp.where(table_lookup == device_id, serial, 0))
    operator_array = polynomial_tables[0]
    parts = jnp.arange(2, dtype=jnp.int32)[None, :]
    column_pick = (2 * wave_of[:, None] + parts).reshape(-1)
    ordered = jnp.take(azimuthal_coeffs, column_pick, axis=2)
    ordered = ordered.reshape(lat_rows, level_cols, band_count, lev_count, 2)
    ordered = jnp.transpose(ordered, (0, 2, 3, 1, 4)).reshape(
        lat_rows, band_count, lev_count * level_cols * 2
    )
    level_mixed = lax.all_to_all(ordered, "lev", split_axis=2, concat_axis=2, tiled=True)
    harmonic_coeffs = analyse_wave(
        lax.all_to_all(level_mixed, "band", split_axis=1, concat_axis=0, tiled=True)[:, 0, :],
        own_wave,
        operator_array,
        gauss_masses,
        circle_samples,
    )
    result = complete_harmonic(
        harmonic_coeffs,
        own_wave,
        operator_array,
        circle_samples,
        eigen_basis,
        basis_mapping,
        eigen_constants,
        hydrostatic_matrix,
        thermal_response,
    )
    returned = lax.all_to_all(
        lax.all_to_all(result[:, None, :], "band", split_axis=0, concat_axis=1, tiled=True),
        "lev",
        split_axis=2,
        concat_axis=2,
        tiled=True,
    )
    returned = returned.reshape(lat_rows, band_count, lev_count, level_cols, 2)
    returned = jnp.transpose(returned, (0, 3, 1, 2, 4)).reshape(lat_rows, level_cols, last_width)
    back_pick = (2 * table_lookup[:, None] + parts).reshape(-1)
    return jnp.take(returned, back_pick, axis=2)


def solution(mesh):
    placed = (
        P("band", "lev", None),
        P(("band", "lev"), None, None, None),
        P(),
        P(),
        P(),
        P(),
        P(),
        P(),
        P(),
        P(),
    )
    return jax.shard_map(
        per_device, mesh=mesh, in_specs=placed, out_specs=P("band", "lev", None), check_vma=False
    )
```

profile of v0, /device:TPU:0, one launch (start us, length us, event | category | flops | bytes accessed | tf_op | source)
XLA Modules:
  0.0 95.0 jit_solution(13781600453538992396)
XLA Ops:
  0.0 1.4 %broadcast_multiply_fusion = (s32[32]{0:T(128)S(1)}, s32[32]{0:T(128)S(1)}, s32[]{:T(128)}) fusion(s32[32]{0:T(128)} %param.16, s32[]{:T(128)S(6)} %add.120), kind=kLoop, calls=%fused_computation.77 | loop fusion | flops 223 | bytes 392 | tf_op jit(solution)/shard_map/mul | solution.py:168
  1.4 0.7 scatter_custom_fusion
  2.1 0.1 add.118
  2.3 2.5 %gather_fusion = bf16[64,640,8]{1,0,2:T(8,128)(2,1)S(1)} fusion(bf16[640,8,64]{0,2,1:T(8,128)(2,1)S(1)} %copy-done, s32[1024]{0:T(1024)S(1)} %pad_clamp_fusion.1), kind=kCustom, calls=%fused_computation.clone | custom fusion | bytes 1310976 | tf_op jit(solution)/shard_map/jit(_take)/gather | solution.py:135
  4.9 0.1 select_bitcast_fusion.1
  5.0 0.2 reshape.147
  5.3 1.1 %copy.64 = bf16[640,8,4,8,2]{0,2,4,1,3:T(4,128)(2,1)} copy(bf16[640,8,4,8,2]{0,4,3,2,1:T(2,128)(2,1)S(1)} %reshape.147) | data formatting | bytes 1310720 | tf_op jit(solution)/shard_map/reshape | solution.py:136
  6.4 7.3 %all-to-all-start = ((bf16[640,4,128]{0,1,2:T(4,128)(2,1)}), bf16[640,4,128]{0,1,2:T(4,128)(2,1)S(1)}, u32[]{:S(2)}, u32[]{:S(2)}) async-start(bf16[640,4,128]{0,1,2:T(4,128)(2,1)} %bitcast.2), calls=%async_computation | async-start | bytes 1310720 | tf_op jit(solution)/shard_map/all_to_all | solution.py:140
  14.3 0.6 multiply_add_fusion.1
  14.9 0.1 fusion.33
  15.1 15.9 %all-to-all-done = bf16[640,4,128]{0,1,2:T(4,128)(2,1)S(1)} async-done(((bf16[640,4,128]{0,1,2:T(4,128)(2,1)}), bf16[640,4,128]{0,1,2:T(4,128)(2,1)S(1)}, u32[]{:S(2)}, u32[]{:S(2)}) %all-to-all-start) | async-done | bytes 655392 | tf_op jit(solution)/shard_map/all_to_all | solution.py:140
  30.9 0.9 copy.65
  31.9 3.5 %all-to-all-start.1 = ((bf16[640,4,128]{0,2,1:T(8,128)(2,1)}), bf16[640,4,128]{0,2,1:T(8,128)(2,1)S(1)}, u32[]{:S(2)}, u32[]{:S(2)}) async-start(bf16[640,4,128]{0,2,1:T(8,128)(2,1)} %copy.65), calls=%async_computation.1 | async-start | bytes 1310720 | tf_op jit(solution)/shard_map/all_to_all | solution.py:142
  35.3 0.6 compare_convert_fusion
  36.1 9.4 %all-to-all-done.1 = bf16[640,4,128]{0,2,1:T(8,128)(2,1)S(1)} async-done(((bf16[640,4,128]{0,2,1:T(8,128)(2,1)}), bf16[640,4,128]{0,2,1:T(8,128)(2,1)S(1)}, u32[]{:S(2)}, u32[]{:S(2)}) %all-to-all-start.1) | async-done | bytes 655392 | tf_op jit(solution)/shard_map/all_to_all | solution.py:142
  45.5 0.3 copy.66
  45.9 0.3 rev.8
  46.3 2.0 %fusion = f32[448,128]{1,0:T(8,128)S(1)} fusion(bf16[1,2,448,1280]{3,2,1,0:T(8,128)(2,1)} %param.13, bf16[1280,128]{1,0:T(8,128)(2,1)S(1)} %rev.8, bf16[1280,128]{1,0:T(8,128)(2,1)S(1)} %bitcast.105, f32[1280]{0:T(1024)S(1)} %broadcast_select_fusion, f32[448]{0:T(512)S(1)} %get-tuple-element.26), kind=kOutput, calls=%fused_computation.5 | convolution fusion | flops 147677184 | bytes 2038528 | tf_op jit(solution)/shard_map/dot_general | solution.py:63
  48.3 0.6 fusion.1
  48.9 0.2 copy.67
  49.1 0.3 reshape.149
  49.5 0.1 copy-done.2
  49.6 0.2 fusion.11
  49.8 0.2 fusion.9
  50.1 0.2 convolution_bitcast_fusion.1
  50.4 0.2 fusion.13
  50.7 0.1 fusion.41
  50.8 0.1 copy.73
  50.9 0.1 slice.56
  51.0 1.6 %fusion.2 = f32[128,1280]{1,0:T(8,128)S(1)} fusion(bf16[448,128]{0,1:T(8,128)(2,1)S(1)} %slice.56, bf16[1,2,448,1280]{3,2,1,0:T(8,128)(2,1)} %param.13), kind=kOutput, calls=%fused_computation.7 | convolution fusion | flops 146800640 | bytes 1916928 | tf_op jit(solution)/shard_map/dot_general | solution.py:103
  52.7 0.1 copy.72
  52.8 0.1 slice.54
  52.9 1.6 %fusion.5 = f32[128,1280]{1,0:T(8,128)S(1)} fusion(bf16[448,128]{0,1:T(8,128)(2,1)S(1)} %slice.54, bf16[1,2,448,1280]{3,2,1,0:T(8,128)(2,1)} %param.13), kind=kOutput, calls=%fused_computation.10 | convolution fusion | flops 146800640 | bytes 1916928 | tf_op jit(solution)/shard_map/dot_general | solution.py:100
  54.7 1.0 %rev.9 = bf16[1280,128]{0,1:T(8,128)(2,1)S(1)} reverse(bf16[1280,128]{0,1:T(8,128)(2,1)S(1)} %multiply_bitcast_fusion), dimensions={0} | reverse | bytes 655360 | tf_op jit(solution)/shard_map/jit(_flip)/rev | solution.py:109
  55.8 0.5 broadcast.172
  56.3 1.1 %reduce = bf16[2560,128]{0,1:T(8,128)(2,1)S(1)} reduce(bf16[2560,1,128]{0,2,1:T(8,128)(2,1)S(1)} %pad_maximum_fusion, bf16[]{:T(256)} %broadcast.172), dimensions={1}, to_apply=%copy.74.reduce_sub_computation | reduce | bytes 1310722 | tf_op jit(solution)/shard_map/concatenate | solution.py:109
  57.4 0.3 copy.96
  57.7 0.2 reshape.190
  57.9 12.6 %all_to_all.43 = bf16[4,2,40960]{2,1,0:T(2,128)(2,1)S(1)} all-to-all(bf16[4,2,40960]{2,1,0:T(2,128)(2,1)S(1)} %reshape.190), channel_id=1, replica_groups=mesh['band'=4,'lev'=8] {'band'}, dimensions={0} | all-to-all | bytes 1310720 | tf_op jit(solution)/shard_map/all_to_all | solution.py:160
  70.5 0.6 reshape.191
  71.1 0.1 copy.78
  71.2 1.3 %copy.75 = bf16[640,4,128]{0,1,2:T(4,128)(2,1)} copy(bf16[640,4,128]{2,0,1:T(8,128)(2,1)S(1)} %bitcast.102) | data formatting | bytes 1310720 | tf_op jit(solution)/shard_map/all_to_all | solution.py:160
  72.5 3.6 %all-to-all-start.3 = ((bf16[640,4,128]{0,1,2:T(4,128)(2,1)}), bf16[640,4,128]{0,1,2:T(4,128)(2,1)S(1)}, u32[]{:S(2)}, u32[]{:S(2)}) async-start(bf16[640,4,128]{0,1,2:T(4,128)(2,1)} %copy.75), calls=%async_computation.3 | async-start | bytes 1310720 | tf_op jit(solution)/shard_map/all_to_all | solution.py:159
  76.2 0.1 add.133
  76.4 16.8 %all-to-all-done.3 = bf16[640,4,128]{0,1,2:T(4,128)(2,1)S(1)} async-done(((bf16[640,4,128]{0,1,2:T(4,128)(2,1)}), bf16[640,4,128]{0,1,2:T(4,128)(2,1)S(1)}, u32[]{:S(2)}, u32[]{:S(2)}) %all-to-all-start.3) | async-done | bytes 655392 | tf_op jit(solution)/shard_map/all_to_all | solution.py:159
  93.3 0.7 gather_fusion.1
  94.0 0.2 select_bitcast_fusion
  94.1 0.9 copy.77
  (40 shorter events, 0.8 us)
Async XLA Ops:
  0.0 2.3 %copy-start = (bf16[640,8,64]{0,2,1:T(8,128)(2,1)S(1)}, bf16[640,8,64]{0,2,1:T(8,128)(2,1)}, u32[]{:S(2)}) copy-start(bf16[640,8,64]{0,2,1:T(8,128)(2,1)} %param.12) | copy-start | bytes 1966084
  5.3 9.8 %copy-start.4 = (s32[1280]{0:T(1024)S(1)}, s32[1280]{0:T(1024)}, u32[]{:S(2)}) copy-start(s32[1280]{0:T(1024)} %param.15) | copy-start | bytes 15364
  6.4 24.6 %all-to-all-start = ((bf16[640,4,128]{0,1,2:T(4,128)(2,1)}), bf16[640,4,128]{0,1,2:T(4,128)(2,1)S(1)}, u32[]{:S(2)}, u32[]{:S(2)}) async-start(bf16[640,4,128]{0,1,2:T(4,128)(2,1)} %bitcast.2), calls=%async_computation | async-start | bytes 1310720 | tf_op jit(solution)/shard_map/all_to_all | solution.py:140
  15.0 21.0 %copy-start.5 = (f32[1280]{0:T(1024)S(1)}, f32[1280]{0:T(1024)}, u32[]{:S(2)}) copy-start(f32[1280]{0:T(1024)} %param.14) | copy-start | bytes 15364
  15.0 21.0 %copy-start.7 = (f32[16]{0:T(128)S(1)}, f32[16]{0:T(128)}, u32[]{:S(2)}) copy-start(f32[16]{0:T(128)} %param.19) | copy-start | bytes 196
  31.9 13.7 %all-to-all-start.1 = ((bf16[640,4,128]{0,2,1:T(8,128)(2,1)}), bf16[640,4,128]{0,2,1:T(8,128)(2,1)S(1)}, u32[]{:S(2)}, u32[]{:S(2)}) async-start(bf16[640,4,128]{0,2,1:T(8,128)(2,1)} %copy.65), calls=%async_computation.1 | async-start | bytes 1310720 | tf_op jit(solution)/shard_map/all_to_all | solution.py:142
  46.3 2.0 %copy-start.1 = (bf16[1,2,448,1280]{3,2,1,0:T(8,128)(2,1)S(1)}, bf16[1,2,448,1280]{3,2,1,0:T(8,128)(2,1)}, u32[]{:S(2)}) copy-start(bf16[1,2,448,1280]{3,2,1,0:T(8,128)(2,1)} %param.13) | copy-start | bytes 6881284
  48.9 0.7 copy-start.2
  49.1 0.7 copy-start.8
  49.1 1.0 %copy-start.6 = (f32[16,16]{1,0:T(8,128)S(1)}, f32[16,16]{1,0:T(8,128)}, u32[]{:S(2)}) copy-start(f32[16,16]{1,0:T(8,128)} %param.17) | copy-start | bytes 3076
  49.1 1.2 %copy-start.3 = (f32[16,16]{1,0:T(8,128)S(1)}, f32[16,16]{1,0:T(8,128)}, u32[]{:S(2)}) copy-start(f32[16,16]{1,0:T(8,128)} %param.21) | copy-start | bytes 3076
  72.5 20.7 %all-to-all-start.3 = ((bf16[640,4,128]{0,1,2:T(4,128)(2,1)}), bf16[640,4,128]{0,1,2:T(4,128)(2,1)S(1)}, u32[]{:S(2)}, u32[]{:S(2)}) async-start(bf16[640,4,128]{0,1,2:T(4,128)(2,1)} %copy.75), calls=%async_computation.3 | async-start | bytes 1310720 | tf_op jit(solution)/shard_map/all_to_all | solution.py:159
where the time goes:
time: 95.6 us; the launch traced here: 95 us
  waiting for transfers between devices  42.2 us (44%)
  starting transfers between devices  14.4 us (15%)
  local copies, waits for them, and re-layouts  13.4 us (14%)
  blocking collectives  12.6 us (13%)
  matrix products  6.71 us (7%)
  other arithmetic  4.69 us (5%)
  between operations  1.12 us (1%)
    all_to_all x1, waiting for transfers between devices, per_device(): lax.all_to_all(lax.all_to_all(result[:, None, :], 'band', split_axis=0, c...  16.8 us
    all_to_all x1, waiting for transfers between devices, per_device(): lax.all_to_all(ordered, 'lev', split_axis=2, concat_axis=2, tiled=True)  15.9 us
    all_to_all x1, blocking collectives, per_device(): lax.all_to_all(result[:, None, :], 'band', split_axis=0, concat_axis=1, t...  12.6 us
    all_to_all x1, waiting for transfers between devices, per_device(): lax.all_to_all(level_mixed, 'band', split_axis=1, concat_axis=0, tiled=True)  9.43 us
    all_to_all x1, starting transfers between devices, per_device(): lax.all_to_all(ordered, 'lev', split_axis=2, concat_axis=2, tiled=True)  7.28 us
    all_to_all x1, starting transfers between devices, per_device(): lax.all_to_all(lax.all_to_all(result[:, None, :], 'band', split_axis=0, c...  3.63 us
    all_to_all x1, starting transfers between devices, per_device(): lax.all_to_all(level_mixed, 'band', split_axis=1, concat_axis=0, tiled=True)  3.48 us
    gather x1, local copies, waits for them, and re-layouts, per_device(): ordered = jnp.take(azimuthal_coeffs, column_pick, axis=2)  2.54 us
  transfers between devices with their start and end apart: 3, of which 3 were waited for; matrix products, arithmetic and copies ran while one was open for 2% of the time, Pallas kernels for 0%

commit v1 on v0

--- a/solution.py
+++ b/solution.py
@@ -156,12 +156,22 @@
         hydrostatic_matrix,
         thermal_response,
     )
-    returned = lax.all_to_all(
-        lax.all_to_all(result[:, None, :], "band", split_axis=0, concat_axis=1, tiled=True),
-        "lev",
-        split_axis=2,
-        concat_axis=2,
-        tiled=True,
+    returned = jnp.concatenate(
+        jax.lax.all_to_all(
+            jnp.stack(
+                jnp.split(
+                    lax.all_to_all(
+                        result[:, None, :], "band", split_axis=0, concat_axis=1, tiled=True
+                    ),
+                    jax.lax.axis_size("lev"),
+                    axis=2,
+                )
+            ),
+            axis_name="lev",
+            split_axis=0,
+            concat_axis=0,
+        ),
+        axis=2,
     )
     returned = returned.reshape(lat_rows, band_count, lev_count, level_cols, 2)
     returned = jnp.transpose(returned, (0, 3, 1, 2, 4)).reshape(lat_rows, level_cols, last_width)

time: 95.6 us -> 113 us (1.18)
  local copies, waits for them, and re-layouts: 13.4 us -> 32.5 us
  matrix products: 6.71 us -> 5.2 us
    another operation x0 -> x8, local copies, waits for them, and re-layouts: none -> 6.71 us  [per_device(): jnp.stack(jnp.split(lax.all_to_all(result[:, None, :], 'band', split_axis...]
    unnamed x22 -> x33, local copies, waits for them, and re-layouts: 1.36 us -> 5.79 us
    split x0 -> x2, local copies, waits for them, and re-layouts: none -> 4.18 us  [per_device(): jnp.split(lax.all_to_all(result[:, None, :], 'band', split_axis=0, concat...]
    rev x1, local copies, waits for them, and re-layouts: 0.34 us -> 3.2 us  [analyse_wave(): south = jnp.flip(column[half_rows:], axis=0).astype(jnp.float32)]
    dot_general x1, matrix products: 0.58 us -> 2.04 us  [analyse_wave(): jnp.dot(operator_array[1], odd_part, preferred_element_type=jnp.float32)]
    dot_general x1, matrix products: 1.61 us -> 0.34 us  [complete_harmonic(): lax.dot_general(operator_array[1], refreshed[pair_rows:], contract, prefe...]
    dot_general x1, matrix products: 1.61 us -> 0.34 us  [complete_harmonic(): lax.dot_general(operator_array[0], refreshed[:pair_rows], contract, prefe...]
  transfers between devices with their start and end apart: 3 -> 3, of which waited for: 3 -> 3; matrix products, arithmetic and copies ran while one was open for 2% -> 1% of each run, Pallas kernels for 0% -> 0%
where the time goes in v1:
time: 113 us
  waiting for transfers between devices  42.6 us (38%)
  local copies, waits for them, and re-layouts  32.5 us (29%)
  starting transfers between devices  14.4 us (13%)
  blocking collectives  12.6 us (11%)
  matrix products  5.2 us (5%)
  other arithmetic  4.51 us (4%)
    all_to_all x1, waiting for transfers between devices, per_device(): jax.lax.all_to_all(jnp.stack(jnp.split(lax.all_to_all(result[:, None, :],...  17 us
    all_to_all x1, waiting for transfers between devices, per_device(): lax.all_to_all(ordered, 'lev', split_axis=2, concat_axis=2, tiled=True)  16 us
    all_to_all x1, blocking collectives, per_device(): lax.all_to_all(result[:, None, :], 'band', split_axis=0, concat_axis=1, t...  12.6 us
    all_to_all x1, waiting for transfers between devices, per_device(): lax.all_to_all(level_mixed, 'band', split_axis=1, concat_axis=0, tiled=True)  9.51 us
    all_to_all x1, starting transfers between devices, per_device(): lax.all_to_all(ordered, 'lev', split_axis=2, concat_axis=2, tiled=True)  7.28 us
    another operation x8, local copies, waits for them, and re-layouts, per_device(): jnp.stack(jnp.split(lax.all_to_all(result[:, None, :], 'band', split_axis...  6.71 us
    unnamed x33, local copies, waits for them, and re-layouts  5.79 us
    split x2, local copies, waits for them, and re-layouts, per_device(): jnp.split(lax.all_to_all(result[:, None, :], 'band', split_axis=0, concat...  4.18 us
  transfers between devices with their start and end apart: 3, of which 3 were waited for; matrix products, arithmetic and copies ran while one was open for 1% of the time, Pallas kernels for 0%

profile of v1, /device:TPU:0, one launch (start us, length us, event | category | flops | bytes accessed | tf_op | source)
XLA Modules:
  0.0 112.8 jit_solution(14515721709049119758)
XLA Ops:
  0.0 1.4 %broadcast_multiply_fusion = (s32[32]{0:T(128)S(1)}, s32[32]{0:T(128)S(1)}, s32[]{:T(128)}) fusion(s32[32]{0:T(128)} %param.16, s32[]{:T(128)S(6)} %add.120), kind=kLoop, calls=%fused_computation.92 | loop fusion | flops 223 | bytes 392 | tf_op jit(solution)/shard_map/mul | solution.py:178
  1.4 0.7 scatter_custom_fusion
  2.5 2.5 %gather_fusion = bf16[64,640,8]{1,0,2:T(8,128)(2,1)S(1)} fusion(bf16[640,8,64]{0,2,1:T(8,128)(2,1)S(1)} %copy-done, s32[1024]{0:T(1024)S(1)} %get-tuple-element.36), kind=kCustom, calls=%fused_computation.clone | custom fusion | bytes 1310976 | tf_op jit(solution)/shard_map/jit(_take)/gather | solution.py:135
  5.2 0.2 reshape.147
  5.4 1.1 copy.88
  6.5 7.3 %all-to-all-start = ((bf16[640,4,128]{0,1,2:T(4,128)(2,1)}), bf16[640,4,128]{0,1,2:T(4,128)(2,1)S(1)}, u32[]{:S(2)}, u32[]{:S(2)}) async-start(bf16[640,4,128]{0,1,2:T(4,128)(2,1)} %bitcast.2), calls=%async_computation | async-start | bytes 1310720 | tf_op jit(solution)/shard_map/all_to_all | solution.py:140
  14.4 0.6 multiply_add_fusion.1
  15.1 16.0 %all-to-all-done = bf16[640,4,128]{0,1,2:T(4,128)(2,1)S(1)} async-done(((bf16[640,4,128]{0,1,2:T(4,128)(2,1)}), bf16[640,4,128]{0,1,2:T(4,128)(2,1)S(1)}, u32[]{:S(2)}, u32[]{:S(2)}) %all-to-all-start) | async-done | bytes 655392 | tf_op jit(solution)/shard_map/all_to_all | solution.py:140
  31.1 0.9 copy.89
  32.0 3.5 %all-to-all-start.1 = ((bf16[640,4,128]{0,2,1:T(8,128)(2,1)}), bf16[640,4,128]{0,2,1:T(8,128)(2,1)S(1)}, u32[]{:S(2)}, u32[]{:S(2)}) async-start(bf16[640,4,128]{0,2,1:T(8,128)(2,1)} %copy.89), calls=%async_computation.1 | async-start | bytes 1310720 | tf_op jit(solution)/shard_map/all_to_all | solution.py:142
  35.5 0.6 compare_convert_fusion
  36.2 9.5 %all-to-all-done.1 = bf16[640,4,128]{0,2,1:T(8,128)(2,1)S(1)} async-done(((bf16[640,4,128]{0,2,1:T(8,128)(2,1)}), bf16[640,4,128]{0,2,1:T(8,128)(2,1)S(1)}, u32[]{:S(2)}, u32[]{:S(2)}) %all-to-all-start.1) | async-done | bytes 655392 | tf_op jit(solution)/shard_map/all_to_all | solution.py:142
  45.7 0.3 copy.90
  46.1 3.2 %rev.8 = bf16[1280,128]{1,0:T(8,128)(2,1)} reverse(bf16[1280,128]{1,0:T(8,128)(2,1)S(1)} %bitcast.122), dimensions={0} | reverse | bytes 655360 | tf_op jit(solution)/shard_map/jit(_flip)/rev | solution.py:59
  49.3 2.0 %fusion.1 = f32[448,128]{1,0:T(8,128)S(1)} fusion(bf16[1,2,448,1280]{3,2,1,0:T(8,128)(2,1)} %param.13, bf16[1280,128]{1,0:T(8,128)(2,1)} %rev.8, bf16[1280,128]{1,0:T(8,128)(2,1)S(1)} %bitcast.124, f32[1280]{0:T(1024)S(1)} %broadcast_select_fusion, f32[448]{0:T(512)S(1)} %get-tuple-element.33), kind=kOutput, calls=%fused_computation.6 | convolution fusion | flops 147677184 | bytes 2038528 | tf_op jit(solution)/shard_map/dot_general | solution.py:64
  51.4 1.5 %fusion = f32[448,128]{1,0:T(8,128)S(1)} fusion(bf16[1,2,448,1280]{3,2,1,0:T(8,128)(2,1)S(1)} %copy-done.1, bf16[1280,128]{1,0:T(8,128)(2,1)} %rev.8, bf16[1280,128]{1,0:T(8,128)(2,1)S(1)} %bitcast.125, f32[1280]{0:T(1024)S(1)} %broadcast_select_fusion, f32[448]{0:T(512)S(1)} %get-tuple-element.34), kind=kOutput, calls=%fused_computation.5 | convolution fusion | flops 147677184 | bytes 2041856 | tf_op jit(solution)/shard_map/dot_general | solution.py:63
  53.0 1.0 copy.91
  54.0 1.3 %reshape.149 = f32[896,4,16,2]{0,3,2,1:T(2,128)S(1)} reshape(f32[896,128]{0,1:T(8,128)} %copy.91) | data formatting | bytes 917504 | tf_op jit(solution)/shard_map/reshape | solution.py:88
  55.4 0.2 fusion.11
  56.1 0.2 fusion.13
  57.1 0.3 fusion.5
  57.4 0.3 fusion.2
  57.9 1.0 rev.9
  59.0 0.5 broadcast.172
  59.5 1.1 reduce
  60.6 0.3 copy.128
  61.1 12.6 %all_to_all.43 = bf16[4,2,40960]{2,1,0:T(2,128)(2,1)S(1)} all-to-all(bf16[4,2,40960]{2,1,0:T(2,128)(2,1)S(1)} %reshape.190), channel_id=1, replica_groups=mesh['band'=4,'lev'=8] {'band'}, dimensions={0} | all-to-all | bytes 1310720 | tf_op jit(solution)/shard_map/all_to_all | solution.py:163
  73.7 0.6 reshape.191
  74.5 2.9 %fusion.39 = (bf16[640,4,16]{2,0,1:T(8,128)(2,1)}, bf16[1,640,4,16]{3,1,2,0:T(8,128)(2,1)}, bf16[1,640,4,16]{3,1,2,0:T(8,128)(2,1)}, bf16[1,640,4,16]{3,1,2,0:T(...) fusion(bf16[640,4,128]{2,0,1:T(8,128)(2,1)S(1)} %bitcast.118), kind=kLoop, calls=%fused_computation.97 | loop fusion | bytes 1310720 | tf_op jit(solution)/shard_map/split | solution.py:162
  77.3 1.3 %copy.99 = bf16[640,4,16]{0,2,1:T(8,128)(2,1)S(1)} copy(bf16[640,4,16]{2,0,1:T(8,128)(2,1)} %get-tuple-element.8) | data formatting | bytes 163840 | tf_op jit(solution)/shard_map/split | solution.py:162
  78.6 1.3 %copy.106 = bf16[1,640,4,16]{1,3,2,0:T(8,128)(2,1)S(1)} copy(bf16[1,640,4,16]{3,1,2,0:T(8,128)(2,1)} %get-tuple-element.9) | data formatting | bytes 163840 | tf_op jit(solution)/shard_map/stack | solution.py:161
  80.0 1.3 %copy.105 = bf16[1,640,4,16]{1,3,2,0:T(8,128)(2,1)S(1)} copy(bf16[1,640,4,16]{3,1,2,0:T(8,128)(2,1)} %get-tuple-element.10) | data formatting | bytes 163840 | tf_op jit(solution)/shard_map/stack | solution.py:161
  81.3 1.9 %copy.104 = bf16[1,640,4,16]{1,3,2,0:T(8,128)(2,1)} copy(bf16[1,640,4,16]{3,1,2,0:T(8,128)(2,1)} %get-tuple-element.11) | data formatting | bytes 163840 | tf_op jit(solution)/shard_map/stack | solution.py:161
  83.2 0.8 copy.103
  84.3 0.2 copy.101
  84.7 0.7 constant_dynamic-update-slice_fusion.6
  85.4 0.6 constant_dynamic-update-slice_fusion.5
  86.0 0.6 constant_dynamic-update-slice_fusion.4
  86.7 0.6 constant_dynamic-update-slice_fusion.3
  87.3 0.6 constant_dynamic-update-slice_fusion.2
  88.0 0.6 constant_dynamic-update-slice_fusion.1
  88.6 0.6 constant_dynamic-update-slice_fusion
  89.2 0.6 bitcast_dynamic-update-slice_fusion
  89.9 3.6 %all-to-all-start.3 = ((bf16[8,640,4,16]{1,3,2,0:T(8,128)(2,1)}), bf16[8,640,4,16]{1,3,2,0:T(8,128)(2,1)S(1)}, u32[]{:S(2)}, u32[]{:S(2)}) async-start(bf16[8,640,4,16]{1,3,2,0:T(8,128)(2,1)} %bitcast_dynamic-update-slice_fusion), calls=%async_computation.3 | async-start | bytes 1310720 | tf_op jit(solution)/shard_map/all_to_all | solution.py:160
  93.5 17.0 %all-to-all-done.3 = bf16[8,640,4,16]{1,3,2,0:T(8,128)(2,1)S(1)} async-done(((bf16[8,640,4,16]{1,3,2,0:T(8,128)(2,1)}), bf16[8,640,4,16]{1,3,2,0:T(8,128)(2,1)S(1)}, u32[]{:S(2)}, u32[]{:S(2)}) %all-to-all-start.3) | async-done | bytes 655392 | tf_op jit(solution)/shard_map/all_to_all | solution.py:160
  110.6 0.4 copy.107
  111.1 0.7 gather_fusion.1
  111.9 0.9 copy.109
  (60 shorter events, 3.2 us)
Async XLA Ops:
  0.0 2.5 %copy-start = (bf16[640,8,64]{0,2,1:T(8,128)(2,1)S(1)}, bf16[640,8,64]{0,2,1:T(8,128)(2,1)}, u32[]{:S(2)}) copy-start(bf16[640,8,64]{0,2,1:T(8,128)(2,1)} %param.12) | copy-start | bytes 1966084
  5.4 9.6 %copy-start.6 = (s32[1280]{0:T(1024)S(1)}, s32[1280]{0:T(1024)}, u32[]{:S(2)}) copy-start(s32[1280]{0:T(1024)} %param.15) | copy-start | bytes 15364
  6.5 24.6 %all-to-all-start = ((bf16[640,4,128]{0,1,2:T(4,128)(2,1)}), bf16[640,4,128]{0,1,2:T(4,128)(2,1)S(1)}, u32[]{:S(2)}, u32[]{:S(2)}) async-start(bf16[640,4,128]{0,1,2:T(4,128)(2,1)} %bitcast.2), calls=%async_computation | async-start | bytes 1310720 | tf_op jit(solution)/shard_map/all_to_all | solution.py:140
  15.0 21.0 %copy-start.7 = (f32[1280]{0:T(1024)S(1)}, f32[1280]{0:T(1024)}, u32[]{:S(2)}) copy-start(f32[1280]{0:T(1024)} %param.14) | copy-start | bytes 15364
  15.1 21.1 %copy-start.9 = (f32[16]{0:T(128)S(1)}, f32[16]{0:T(128)}, u32[]{:S(2)}) copy-start(f32[16]{0:T(128)} %param.19) | copy-start | bytes 196
  32.0 13.7 %all-to-all-start.1 = ((bf16[640,4,128]{0,2,1:T(8,128)(2,1)}), bf16[640,4,128]{0,2,1:T(8,128)(2,1)S(1)}, u32[]{:S(2)}, u32[]{:S(2)}) async-start(bf16[640,4,128]{0,2,1:T(8,128)(2,1)} %copy.89), calls=%async_computation.1 | async-start | bytes 1310720 | tf_op jit(solution)/shard_map/all_to_all | solution.py:142
  49.3 2.1 %copy-start.1 = (bf16[1,2,448,1280]{3,2,1,0:T(8,128)(2,1)S(1)}, bf16[1,2,448,1280]{3,2,1,0:T(8,128)(2,1)}, u32[]{:S(2)}) copy-start(bf16[1,2,448,1280]{3,2,1,0:T(8,128)(2,1)} %param.13) | copy-start | bytes 6881284
  53.0 2.4 %copy-start.4 = (f32[16,16]{1,0:T(8,128)S(1)}, f32[16,16]{1,0:T(8,128)}, u32[]{:S(2)}) copy-start(f32[16,16]{1,0:T(8,128)} %param.20) | copy-start | bytes 3076
  54.0 1.7 %copy-start.10 = (f32[16,16]{1,0:T(8,128)S(1)}, f32[16,16]{1,0:T(8,128)}, u32[]{:S(2)}) copy-start(f32[16,16]{1,0:T(8,128)} %param.18) | copy-start | bytes 3076
  54.0 1.9 %copy-start.8 = (f32[16,16]{1,0:T(8,128)S(1)}, f32[16,16]{1,0:T(8,128)}, u32[]{:S(2)}) copy-start(f32[16,16]{1,0:T(8,128)} %param.17) | copy-start | bytes 3076
  54.0 2.2 %copy-start.5 = (f32[16,16]{1,0:T(8,128)S(1)}, f32[16,16]{1,0:T(8,128)}, u32[]{:S(2)}) copy-start(f32[16,16]{1,0:T(8,128)} %param.21) | copy-start | bytes 3076
  84.0 2.6 %copy-start.3 = (bf16[1,640,4,16]{1,3,2,0:T(8,128)(2,1)S(1)}, bf16[1,640,4,16]{1,3,2,0:T(8,128)(2,1)}, u32[]{:S(2)}) copy-start(bf16[1,640,4,16]{1,3,2,0:T(8,128)(2,1)} %copy.103) | copy-start | bytes 245764
  84.0 3.3 %copy-start.2 = (bf16[1,640,4,16]{1,3,2,0:T(8,128)(2,1)S(1)}, bf16[1,640,4,16]{1,3,2,0:T(8,128)(2,1)}, u32[]{:S(2)}) copy-start(bf16[1,640,4,16]{1,3,2,0:T(8,128)(2,1)} %copy.104) | copy-start | bytes 245764
  89.9 20.7 %all-to-all-start.3 = ((bf16[8,640,4,16]{1,3,2,0:T(8,128)(2,1)}), bf16[8,640,4,16]{1,3,2,0:T(8,128)(2,1)S(1)}, u32[]{:S(2)}, u32[]{:S(2)}) async-start(bf16[8,640,4,16]{1,3,2,0:T(8,128)(2,1)} %bitcast_dynamic-update-slice_fusion), calls=%async_computation.3 | async-start | bytes 1310720 | tf_op jit(solution)/shard_map/all_to_all | solution.py:160
